TPU v7x, 256 devices: a whole 4x4x8 slice. The times are simulated.
256 devices in a mesh: group: 4 (over z_hi), dp: 8 (over y, z_lo), mp: 8 (over x, core).
Axes of the slice: x: 4, y: 4, z: 8 (z_hi: 4, z_lo: 2; z = z_hi * 2 + z_lo), core: 2. Of those that a mesh axis runs over, the one named last changes fastest.
Arguments:
- inner_columns: float32 [4, 576, 4032], P('group', None, 'mp'), may hold values from -6 to 6
- inner_rows: float32 [4, 2112, 576], P('group', 'mp'), may hold values from -6 to 6
- inner_norms: float32 [4, 3, 576], P('group'), may hold values from -6 to 6
- inner_embed: float32 [4, 8192, 576], P('group', 'mp'), may hold values from -6 to 6
- basis: float32 [576, 64], replicated, may hold values from -0.25 to 0.25
- outer_layer: float32 [8, 442368], P('mp', ('group', 'dp')), may hold values from -6 to 6
- outer_norms: float32 [1728], P(('group', 'dp')), may hold values from -6 to 6
- outer_embed: float32 [8, 1024, 576], P('mp', ('group', 'dp')), may hold values from -6 to 6
- layer_momentum: float32 [8, 442368], P('mp', ('group', 'dp')), may hold values from -6 to 6
- norm_momentum: float32 [1728], P(('group', 'dp')), may hold values from -6 to 6
- embed_momentum: float32 [8, 1024, 576], P('mp', ('group', 'dp')), may hold values from -6 to 6
Outputs:
- new_columns: float32 [576, 4032], P(None, 'mp')
- new_rows: float32 [2112, 576], P('mp')
- new_norms: float32 [3, 576], replicated
- new_embed: float32 [8192, 576], P('mp')
- new_layer_momentum: float32 [8, 442368], P('mp', ('group', 'dp'))
- new_norm_momentum: float32 [1728], P(('group', 'dp'))
- new_embed_momentum: float32 [8, 1024, 576], P('mp', ('group', 'dp'))
All inputs are finite; a program needn't handle non-finite values.
Results may differ from a plain program's by a relative error of at most 0.000076.
Values sent between devices are 32-bit elements; how exact they have to be, the bound alone decides.
No kernel may reach another device: no remote copies, remote signals or barrier semaphores. Data moves between devices by JAX's collectives and lax.ppermute only.
A program may use at most 64 MiB of HBM per device.

v0:
```python
import jax
import jax.numpy as jnp
from jax import lax
from jax.sharding import PartitionSpec as P

MU = 0.5
RATE = 0.7


def nesterov(weights, delta, momentum):
    fresh = MU * momentum + delta
    return (weights - RATE * (delta + MU * fresh), fresh)


def local(
    inner_columns,
    inner_rows,
    inner_norms,
    inner_embed,
    basis,
    outer_layer,
    outer_norms,
    outer_embed,
    layer_momentum,
    norm_momentum,
    embed_momentum,
):
    groups = lax.axis_size("group")
    copies = lax.axis_size("dp")
    place = lax.axis_index("dp")
    width = inner_columns.shape[1]
    col_width = inner_columns.shape[2]

    def own_pieces(flat):
        table = flat.reshape(groups, copies, -1)
        return lax.dynamic_index_in_dim(table, place, 1, keepdims=False)

    layer_pieces = own_pieces(
        jnp.concatenate([inner_columns[0].reshape(-1), inner_rows[0].reshape(-1)])
    )
    norm_pieces = own_pieces(inner_norms[0].reshape(-1))
    embed_rows = inner_embed[0]
    row_table = embed_rows.reshape(groups, copies, -1, width)
    row_pieces = lax.dynamic_index_in_dim(row_table, place, 1, keepdims=False)
    outer_rows = outer_embed[0]
    layer_sum, norm_sum, rows_sum = (
        lax.psum_scatter(layer_pieces, "group", scatter_dimension=0, tiled=True),
        lax.psum_scatter(norm_pieces, "group", scatter_dimension=0, tiled=True),
        lax.psum_scatter(row_pieces, "group", scatter_dimension=0, tiled=True),
    )
    factor = jnp.dot(
        outer_rows - rows_sum[0] / groups,
        basis,
        precision=lax.Precision.HIGHEST,
        preferred_element_type=jnp.float32,
    )
    embed_delta = jnp.dot(
        factor, basis.T, precision=lax.Precision.HIGHEST, preferred_element_type=jnp.float32
    )
    outer_piece = outer_layer[0]
    new_layer, new_layer_m = nesterov(
        outer_piece, outer_piece - layer_sum[0] / groups, layer_momentum[0]
    )
    new_norm, new_norm_m = nesterov(outer_norms, outer_norms - norm_sum[0] / groups, norm_momentum)
    new_embed_rows, new_embed_m = nesterov(outer_rows, embed_delta, embed_momentum[0])
    pieces = (new_layer[None, :], new_norm[None, :], new_embed_rows)
    layer_all, norm_all, embed_all = (
        lax.all_gather(pieces[0], ("group", "dp"), axis=0, tiled=True),
        lax.all_gather(pieces[1], ("group", "dp"), axis=0, tiled=True),
        lax.all_gather(pieces[2], ("group", "dp"), axis=0, tiled=True),
    )
    layer_whole = layer_all.reshape(-1)
    split = width * col_width
    new_columns = layer_whole[:split].reshape(width, col_width)
    new_rows = layer_whole[split:].reshape(-1, width)
    new_norms = norm_all.reshape(3, width)
    return (
        new_columns,
        new_rows,
        new_norms,
        embed_all,
        new_layer_m[None, :],
        new_norm_m,
        new_embed_m[None, :, :],
    )


def solution(mesh):
    in_specs = (
        P("group", None, "mp"),
        P("group", "mp", None),
        P("group", None, None),
        P("group", "mp", None),
        P(),
        P("mp", ("group", "dp")),
        P(("group", "dp")),
        P("mp", ("group", "dp"), None),
        P("mp", ("group", "dp")),
        P(("group", "dp")),
        P("mp", ("group", "dp"), None),
    )
    out_specs = (
        P(None, "mp"),
        P("mp", None),
        P(),
        P("mp", None),
        P("mp", ("group", "dp")),
        P(("group", "dp")),
        P("mp", ("group", "dp"), None),
    )
    return jax.shard_map(local, mesh=mesh, in_specs=in_specs, out_specs=out_specs, check_vma=False)
```

profile of v0, /device:TPU:6, one launch (start us, length us, event | category | flops | bytes accessed | tf_op | source)
XLA Modules:
  0.0 396.3 jit_solution(6770101458662133229)
XLA Ops:
  7.2 0.0 copy-start
  7.2 0.0 copy-start.2
  7.2 0.0 all-reduce.5.cloned.1.call-start
  7.2 2.3 reshape_squeeze.10
  9.6 0.0 copy-done.2
  9.6 1.1 reshape_squeeze.9
  10.7 1.2 pad_maximum_fusion
  11.9 1.7 reshape.37
  13.5 1.6 constant_dynamic-slice_fusion.2
  15.2 0.7 copy.28
  15.9 0.0 all-reduce.5.cloned.1.call-update
  15.9 0.0 copy-start.11
  15.9 0.0 copy-start.5
  16.0 0.0 copy-start.6
  16.0 0.0 copy-start.3
  16.0 0.0 copy-start.4
  16.0 0.0 reduce-scatter.2.cloned.1.call-start
  16.0 2.1 copy.23
  18.2 0.0 copy-start.7
  18.2 0.0 copy-start.10
  18.2 0.0 copy-start.8
  18.2 0.0 copy-start.9
  18.2 0.8 dynamic-slice_bitcast_fusion
  19.0 0.0 reduce-scatter.2.cloned.1.call-update
  19.0 0.0 all-gather.7.cloned.1.call-start
  19.1 0.6 dynamic-slice.1
  19.7 50.2 %all-reduce.5.cloned.1.call-done = f32[4,13824]{1,0:T(4,128)} async-done(((f32[4,13824]{1,0:T(4,128)}), f32[4,13824]{1,0:T(4,128)}) %all-reduce.5.cloned.1.call-update) | async-done | bytes 221200
  69.9 2.4 subtract_bitcast_fusion
  72.2 0.0 all-gather.7.cloned.1.call-update
  72.3 0.0 all-gather.5.cloned.1.call-start
  72.3 25.3 %reduce-scatter.2.cloned.1.call-done = f32[1,32,576]{2,1,0:T(8,128)} async-done(((f32[4,32,576]{2,1,0:T(8,128)}), f32[1,32,576]{2,1,0:T(8,128)}) %reduce-scatter.2.cloned.1.call-update) | async-done | bytes 73744 | tf_op jit(solution)/shard_map/reduce_scatter | solution.py:49
  97.6 1.2 fusion
  98.7 0.0 copy-done.4
  98.8 0.9 fusion.3
  99.7 0.0 all-gather.5.cloned.1.call-update
  99.7 0.1 reshape_reshape_squeeze.3
  99.8 0.6 dynamic-slice
  101.1 11.7 %all-reduce.2 = f32[4,54]{1,0:T(4,128)S(1)} all-reduce(f32[4,54]{1,0:T(4,128)S(1)} %bitcast.44), channel_id=4, replica_groups=mesh['group'=4,'dp'=8,'mp'=8] {'group'}, use_global_device_ids=true, to_apply=%region_1.2.clone | all-reduce | flops 216 | bytes 1728
  112.8 1.2 subtract_dynamic-update-slice_fusion
  114.0 73.0 %all-reduce = f32[1728]{0:T(1024)S(1)} all-reduce(f32[1728]{0:T(1024)S(1)} %get-tuple-element.28), channel_id=2, replica_groups=mesh['group'=4,'dp'=8,'mp'=8] {'group','dp'}, use_global_device_ids=true, to_apply=%add | all-reduce | flops 1728 | bytes 13824
  187.0 0.7 reshape.40
  187.7 54.7 %all-gather.7.cloned.1.call-done = f32[32,1,13824]{2,1,0:T(1,128)} async-done(((f32[1,1,13824]{2,1,0:T(1,128)}), f32[32,1,13824]{2,1,0:T(1,128)}) %all-gather.7.cloned.1.call-update) | async-done | bytes 1769488 | tf_op jit(solution)/shard_map/all_gather | solution.py:68
  242.4 2.8 slice_reduce_fusion.1
  245.1 1.1 reshape.39
  246.2 3.0 slice_reduce_fusion
  249.2 2.4 reshape.38
  251.5 135.1 %all-gather.5.cloned.1.call-done = f32[1024,576]{1,0:T(8,128)} async-done(((f32[32,576]{1,0:T(8,128)}), f32[1024,576]{1,0:T(8,128)}) %all-gather.5.cloned.1.call-update) | async-done | bytes 2359312 | tf_op jit(solution)/shard_map/all_gather | solution.py:70
  386.7 3.1 copy.24
  (14 shorter events, 0.1 us)
Async XLA Ops:
  7.2 90.4 %copy-start = (f32[576,64]{0,1:T(8,128)S(1)}, f32[576,64]{0,1:T(8,128)}, u32[]{:S(2)}) copy-start(f32[576,64]{0,1:T(8,128)} %param.15) | copy-start | bytes 442372
  7.2 2.4 copy-start.2
  7.2 62.7 %all-reduce.5.cloned.1.call-start = ((), (), s32[]{:S(2)}) async-start(), calls=%async_computation.4 | async-start | bytes 442368
  15.9 3.1 copy-start.11
  15.9 53.9 %copy-start.5 = (f32[1,13824]{1,0:T(1,128)S(1)}, f32[1,13824]{1,0:T(1,128)}, u32[]{:S(2)}) copy-start(f32[1,13824]{1,0:T(1,128)} %param.16) | copy-start | bytes 165892
  16.0 53.9 %copy-start.6 = (f32[1,13824]{1,0:T(1,128)S(1)}, f32[1,13824]{1,0:T(1,128)}, u32[]{:S(2)}) copy-start(f32[1,13824]{1,0:T(1,128)} %param.19) | copy-start | bytes 165892
  16.0 81.6 %copy-start.3 = (f32[1,32,576]{2,1,0:T(8,128)S(1)}, f32[1,32,576]{2,1,0:T(8,128)}, u32[]{:S(2)}) copy-start(f32[1,32,576]{2,1,0:T(8,128)} %param.18) | copy-start | bytes 221188
  16.0 82.8 %copy-start.4 = (f32[1,32,576]{2,1,0:T(8,128)S(1)}, f32[1,32,576]{2,1,0:T(8,128)}, u32[]{:S(2)}) copy-start(f32[1,32,576]{2,1,0:T(8,128)} %param.21) | copy-start | bytes 221188
  16.0 81.6 %reduce-scatter.2.cloned.1.call-start = ((), (), s32[]{:S(2)}) async-start(), calls=%async_computation.1 | async-start | bytes 409600 | tf_op jit(solution)/shard_map/reduce_scatter | solution.py:49
  18.2 81.5 %copy-start.7 = (f32[1,3,576]{2,0,1:T(1,128)S(1)}, f32[1,3,576]{2,0,1:T(1,128)}, u32[]{:S(2)}) copy-start(f32[1,3,576]{2,0,1:T(1,128)} %param.13) | copy-start | bytes 20740
  18.2 81.6 %copy-start.10 = (u32[256]{0:T(256)S(1)}, u32[256]{0:T(256)}, u32[]{:S(2)}) copy-start(u32[256]{0:T(256)} %constant.46) | copy-start | bytes 3076
  18.2 94.5 %copy-start.8 = (f32[54]{0:T(128)S(1)}, f32[54]{0:T(128)}, u32[]{:S(2)}) copy-start(f32[54]{0:T(128)} %param.17) | copy-start | bytes 652
  18.2 94.5 %copy-start.9 = (f32[54]{0:T(128)S(1)}, f32[54]{0:T(128)}, u32[]{:S(2)}) copy-start(f32[54]{0:T(128)} %param.20) | copy-start | bytes 652
  19.0 223.3 %all-gather.7.cloned.1.call-start = ((), (), s32[]{:S(2)}) async-start(), calls=%async_computation.3 | async-start | bytes 1824768 | tf_op jit(solution)/shard_map/all_gather | solution.py:68
  72.3 314.4 %all-gather.5.cloned.1.call-start = ((), (), s32[]{:S(2)}) async-start(), calls=%async_computation.2 | async-start | bytes 2703360 | tf_op jit(solution)/shard_map/all_gather | solution.py:70
  242.4 3.8 copy-start.1
Sparse Core Ops, SparseCore 0:
  16.1 53.7 all-reduce.4
  72.9 24.5 reduce-scatter.1
  99.9 142.3 all-gather.6
  244.6 142.0 all-gather.4
where the time goes:
time: 397 us; the launch traced here: 396 us
  waiting for transfers between devices  265 us (67%)
  blocking collectives  84.7 us (21%)
  local copies, waits for them, and re-layouts  24.7 us (6%)
  between operations  14.6 us (4%)
  other arithmetic  4.81 us (1%)
    all_gather x1, waiting for transfers between devices, local(): lax.all_gather(pieces[2], ('group', 'dp'), axis=0, tiled=True)  135 us
    unnamed x2, blocking collectives  84.7 us
    all_gather x1, waiting for transfers between devices, local(): lax.all_gather(pieces[0], ('group', 'dp'), axis=0, tiled=True)  54.7 us
    unnamed x5, waiting for transfers between devices  50.2 us
    reduce_scatter x1, waiting for transfers between devices, local(): lax.psum_scatter(row_pieces, 'group', scatter_dimension=0, tiled=True)  25.3 us
  transfers between devices with their start and end apart: 4, of which 4 were waited for; matrix products, arithmetic and copies ran while one was open for 5% of the time, Pallas kernels for 0%

commit v1 on v0

--- a/solution.py
+++ b/solution.py
@@ -67,7 +67,12 @@
     layer_all, norm_all, embed_all = (
         lax.all_gather(pieces[0], ("group", "dp"), axis=0, tiled=True),
         lax.all_gather(pieces[1], ("group", "dp"), axis=0, tiled=True),
-        lax.all_gather(pieces[2], ("group", "dp"), axis=0, tiled=True),
+        jnp.concatenate(
+            lax.all_to_all(
+                jnp.stack([pieces[2]] * lax.axis_size(("group", "dp"))), ("group", "dp"), 0, 0
+            ),
+            axis=0,
+        ),
     )
     layer_whole = layer_all.reshape(-1)
     split = width * col_width

time: 397 us -> 271 us (0.68)
  waiting for transfers between devices: 265 us -> 120 us
  starting transfers between devices: 0.16 us -> 7.72 us
  blocking collectives: 84.7 us -> 91.3 us
  local copies, waits for them, and re-layouts: 24.7 us -> 29.8 us
    all_gather x1 -> x0, waiting for transfers between devices: 135 us -> none  [local(): lax.all_gather(pieces[2], ('group', 'dp'), axis=0, tiled=True)]
    all_to_all x0 -> x1, starting transfers between devices: none -> 7.6 us  [local(): lax.all_to_all(jnp.stack([pieces[2]] * lax.axis_size(('group', 'dp'))), (...]
    unnamed x2, blocking collectives: 84.7 us -> 91.3 us
    all_gather x1, waiting for transfers between devices: 54.7 us -> 50.5 us  [local(): lax.all_gather(pieces[0], ('group', 'dp'), axis=0, tiled=True)]
    unnamed x5 -> x4, waiting for transfers between devices: 50.2 us -> 47.9 us
  transfers between devices with their start and end apart: 4 -> 4, of which waited for: 4 -> 3; matrix products, arithmetic and copies ran while one was open for 5% -> 12% of each run, Pallas kernels for 0% -> 0%
where the time goes in v1:
time: 271 us; the launch traced here: 270 us
  waiting for transfers between devices  120 us (44%)
  blocking collectives  91.3 us (34%)
  local copies, waits for them, and re-layouts  29.8 us (11%)
  between operations  14.6 us (5%)
  starting transfers between devices  7.72 us (3%)
  other arithmetic  4.81 us (2%)
    unnamed x2, blocking collectives  91.3 us
    all_gather x1, waiting for transfers between devices, local(): lax.all_gather(pieces[0], ('group', 'dp'), axis=0, tiled=True)  50.5 us
    unnamed x4, waiting for transfers between devices  47.9 us
    reduce_scatter x1, waiting for transfers between devices, local(): lax.psum_scatter(row_pieces, 'group', scatter_dimension=0, tiled=True)  21.6 us
    all_to_all x1, starting transfers between devices, local(): lax.all_to_all(jnp.stack([pieces[2]] * lax.axis_size(('group', 'dp'))), (...  7.6 us
    unnamed x30, local copies, waits for them, and re-layouts  6.18 us
  transfers between devices with their start and end apart: 4, of which 3 were waited for; matrix products, arithmetic and copies ran while one was open for 12% of the time, Pallas kernels for 0%

profile of v1, /device:TPU:6, one launch (start us, length us, event | category | flops | bytes accessed | tf_op | source)
XLA Modules:
  0.0 270.2 jit_solution(345085248202903525)
XLA Ops:
  7.2 0.0 copy-start
  7.2 0.0 reduce-scatter.2.cloned.1.call-start
  7.2 2.2 copy.23
  9.4 0.8 dynamic-slice_bitcast_fusion
  10.2 0.0 reduce-scatter.2.cloned.1.call-update
  10.2 0.0 all-reduce.5.cloned.1.call-start
  10.3 0.0 copy-done.2
  10.3 1.1 reshape_squeeze.10
  11.4 0.0 copy-done.1
  11.5 1.1 reshape_squeeze.9
  12.6 1.2 pad_maximum_fusion
  13.7 0.0 copy-start.11
  13.8 0.0 copy-start.3
  13.8 0.0 copy-start.4
  13.8 1.7 reshape.42
  15.5 1.6 constant_dynamic-slice_fusion.2
  17.1 0.7 copy.28
  17.8 0.0 all-reduce.5.cloned.1.call-update
  17.9 0.6 dynamic-slice.1
  18.5 21.6 %reduce-scatter.2.cloned.1.call-done = f32[1,32,576]{2,1,0:T(8,128)} async-done(((f32[4,32,576]{2,1,0:T(8,128)}), f32[1,32,576]{2,1,0:T(8,128)}) %reduce-scatter.2.cloned.1.call-update) | async-done | bytes 73744 | tf_op jit(solution)/shard_map/reduce_scatter | solution.py:49
  40.0 0.0 copy-done.3
  40.0 1.2 fusion
  41.2 0.0 copy-done.4
  41.2 0.9 fusion.3
  42.1 1.8 stack.2
  43.9 0.0 copy-start.8
  43.9 0.0 copy-start.9
  43.9 7.6 %all-to-all-start = ((f32[32,32,576]{2,1,0:T(8,128)}), f32[32,32,576]{2,1,0:T(8,128)S(1)}, u32[]{:S(2)}, u32[]{:S(2)}) async-start(f32[32,32,576]{2,1,0:T(8,128)} %stack.2), calls=%async_computation.1 | async-start | bytes 5242880 | tf_op jit(solution)/shard_map/all_to_all | solution.py:71
  51.5 0.0 all-gather.4.cloned.1.call-start
  51.6 47.8 %all-reduce.5.cloned.1.call-done = f32[4,13824]{1,0:T(4,128)} async-done(((f32[4,13824]{1,0:T(4,128)}), f32[4,13824]{1,0:T(4,128)}) %all-reduce.5.cloned.1.call-update) | async-done | bytes 221200
  99.4 0.0 copy-done.5
  99.4 2.4 subtract_bitcast_fusion
  101.8 0.0 all-gather.4.cloned.1.call-update
  101.8 0.0 copy-done.7
  101.9 0.1 reshape_reshape_squeeze.3
  102.0 0.6 dynamic-slice
  103.2 17.9 %all-reduce.2 = f32[4,54]{1,0:T(4,128)S(1)} all-reduce(f32[4,54]{1,0:T(4,128)S(1)} %bitcast.46), channel_id=4, replica_groups=mesh['group'=4,'dp'=8,'mp'=8] {'group'}, use_global_device_ids=true, to_apply=%region_1.2.clone | all-reduce | flops 216 | bytes 1728
  121.1 0.0 copy-done.9
  121.1 1.2 subtract_dynamic-update-slice_fusion
  122.3 73.4 %all-reduce = f32[1728]{0:T(1024)S(1)} all-reduce(f32[1728]{0:T(1024)S(1)} %get-tuple-element.21), channel_id=2, replica_groups=mesh['group'=4,'dp'=8,'mp'=8] {'group','dp'}, use_global_device_ids=true, to_apply=%add | all-reduce | flops 1728 | bytes 13824
  195.7 0.7 reshape.45
  196.4 50.5 %all-gather.4.cloned.1.call-done = f32[32,1,13824]{2,1,0:T(1,128)} async-done(((f32[1,1,13824]{2,1,0:T(1,128)}), f32[32,1,13824]{2,1,0:T(1,128)}) %all-gather.4.cloned.1.call-update) | async-done | bytes 1769488 | tf_op jit(solution)/shard_map/all_gather | solution.py:68
  246.9 3.6 %slice_reduce_fusion.1 = f32[11,13824]{1,0:T(8,128)} fusion(f32[32,1,13824]{2,1,0:T(1,128)} %all-gather.4.cloned.1.call-done), kind=kLoop, calls=%fused_computation.2 | loop fusion | bytes 1216512 | tf_op jit(solution)/shard_map/slice | solution.py:80
  250.5 2.2 reshape.44
  252.7 5.3 %slice_reduce_fusion = f32[21,13824]{1,0:T(8,128)} fusion(f32[32,1,13824]{2,1,0:T(1,128)} %all-gather.4.cloned.1.call-done), kind=kLoop, calls=%fused_computation.1 | loop fusion | bytes 2322432 | tf_op jit(solution)/shard_map/slice | solution.py:79
  258.1 3.6 %reshape.43 = f32[576,504]{1,0:T(8,128)} reshape(f32[21,13824]{1,0:T(8,128)} %slice_reduce_fusion) | data formatting | bytes 2322432 | tf_op jit(solution)/shard_map/reshape | solution.py:79
  261.7 0.0 all-to-all-done
  261.7 2.0 copy.24
  (14 shorter events, 0.1 us)
Async XLA Ops:
  7.2 32.9 %copy-start = (f32[576,64]{0,1:T(8,128)S(1)}, f32[576,64]{0,1:T(8,128)}, u32[]{:S(2)}) copy-start(f32[576,64]{0,1:T(8,128)} %param.15) | copy-start | bytes 442372
  7.2 32.8 %reduce-scatter.2.cloned.1.call-start = ((), (), s32[]{:S(2)}) async-start(), calls=%async_computation.2 | async-start | bytes 409600 | tf_op jit(solution)/shard_map/reduce_scatter | solution.py:49
  7.2 3.0 %copy-start.2 = (f32[1,264,576]{2,1,0:T(8,128)S(1)}, f32[1,264,576]{2,1,0:T(8,128)}, u32[]{:S(2)}) copy-start(f32[1,264,576]{2,1,0:T(8,128)} %param.12) | copy-start | bytes 1824772
  10.2 1.3 copy-start.1
  10.2 89.2 %all-reduce.5.cloned.1.call-start = ((), (), s32[]{:S(2)}) async-start(), calls=%async_computation.4 | async-start | bytes 442368
  13.7 4.1 %copy-start.11 = (u32[256]{0:T(256)S(1)}, u32[256]{0:T(256)}, u32[]{:S(2)}) copy-start(u32[256]{0:T(256)} %constant.52) | copy-start | bytes 3076
  13.8 26.3 %copy-start.3 = (f32[1,32,576]{2,1,0:T(8,128)S(1)}, f32[1,32,576]{2,1,0:T(8,128)}, u32[]{:S(2)}) copy-start(f32[1,32,576]{2,1,0:T(8,128)} %param.18) | copy-start | bytes 221188
  13.8 27.4 %copy-start.4 = (f32[1,32,576]{2,1,0:T(8,128)S(1)}, f32[1,32,576]{2,1,0:T(8,128)}, u32[]{:S(2)}) copy-start(f32[1,32,576]{2,1,0:T(8,128)} %param.21) | copy-start | bytes 221188
  43.9 55.5 %copy-start.5 = (f32[1,13824]{1,0:T(1,128)S(1)}, f32[1,13824]{1,0:T(1,128)}, u32[]{:S(2)}) copy-start(f32[1,13824]{1,0:T(1,128)} %param.16) | copy-start | bytes 165892
  43.9 55.5 %copy-start.6 = (f32[1,13824]{1,0:T(1,128)S(1)}, f32[1,13824]{1,0:T(1,128)}, u32[]{:S(2)}) copy-start(f32[1,13824]{1,0:T(1,128)} %param.19) | copy-start | bytes 165892
  43.9 57.9 %copy-start.7 = (f32[1,3,576]{2,0,1:T(1,128)S(1)}, f32[1,3,576]{2,0,1:T(1,128)}, u32[]{:S(2)}) copy-start(f32[1,3,576]{2,0,1:T(1,128)} %param.13) | copy-start | bytes 20740
  43.9 58.1 %copy-start.10 = (u32[256]{0:T(256)S(1)}, u32[256]{0:T(256)}, u32[]{:S(2)}) copy-start(u32[256]{0:T(256)} %constant.46) | copy-start | bytes 3076
  43.9 77.2 %copy-start.8 = (f32[54]{0:T(128)S(1)}, f32[54]{0:T(128)}, u32[]{:S(2)}) copy-start(f32[54]{0:T(128)} %param.17) | copy-start | bytes 652
  43.9 77.2 %copy-start.9 = (f32[54]{0:T(128)S(1)}, f32[54]{0:T(128)}, u32[]{:S(2)}) copy-start(f32[54]{0:T(128)} %param.20) | copy-start | bytes 652
  43.9 217.8 %all-to-all-start = ((f32[32,32,576]{2,1,0:T(8,128)}), f32[32,32,576]{2,1,0:T(8,128)S(1)}, u32[]{:S(2)}, u32[]{:S(2)}) async-start(f32[32,32,576]{2,1,0:T(8,128)} %stack.2), calls=%async_computation.1 | async-start | bytes 5242880 | tf_op jit(solution)/shard_map/all_to_all | solution.py:71
  51.5 195.4 %all-gather.4.cloned.1.call-start = ((), (), s32[]{:S(2)}) async-start(), calls=%async_computation.3 | async-start | bytes 1824768 | tf_op jit(solution)/shard_map/all_gather | solution.py:68
Sparse Core Ops, SparseCore 0:
  11.1 28.8 reduce-scatter.1
  43.2 56.1 all-reduce.4
  101.9 144.9 all-gather.3
